TPU v7x, 256 devices: a whole 4x4x8 slice. The times are simulated.
256 devices in a mesh: rows: 8 (over z), vocab: 32 (over y, x, core).
Axes of the slice: x: 4, y: 4, z: 8, core: 2. Of those that a mesh axis runs over, the one named last changes fastest.
Arguments:
- hidden: bfloat16 [1024, 8192], P('rows', 'vocab'), may hold values from -30 to 30
- head: bfloat16 [8192, 152064], P(None, ('vocab', 'rows')), may hold values from -1 to 1
- states: int32 [1024], replicated, may hold values from 0 to 2047
- class_of: int32 [152064], P('vocab'), may hold values from 0 to 255, as said below
- table: int32 [2048, 8], replicated, may hold values from -2147483648 to 2147483646, as said below
Outputs:
- log_probs: float32 [1024, 152064], P('rows', 'vocab')
- entropy: float32 [1024], P('rows')
Inputs may be any that keep to these rules, and one draw needn't show every extreme that they name: `class_of`: class 0 is the class of at least one token. `table`: bit 0 of word 0 is set in every state, so class 0 is allowed everywhere.
All inputs are finite; a program needn't handle non-finite values.
Results may differ from a plain program's by a relative error of at most 0.0003.
Values may be sent and summed in bfloat16 or wider, within the bound.
No kernel may reach another device: no remote copies, remote signals or barrier semaphores. Data moves between devices by JAX's collectives and lax.ppermute only.
A program may use at most 128 MiB of HBM per device.

v0:
```python
import jax
import jax.numpy as jnp
from jax import lax
from jax.sharding import PartitionSpec as P

masked_floor = -1e30


def from_everyone(shard, axis):
    copies = jnp.broadcast_to(shard, (lax.axis_size(axis), *shard.shape))
    return lax.all_to_all(copies, axis, split_axis=0, concat_axis=0, tiled=True)


def collected_together(shard, axis):
    leaves = jax.tree.leaves(shard)
    sequence = sorted(range(len(leaves)), key=lambda k: -leaves[k].size)
    width = (1, *leaves[sequence[0]].shape)[-1]
    lines = [
        jnp.pad(leaves[k].reshape(-1), (0, -leaves[k].size % width)).reshape(-1, width)
        for k in sequence
    ]
    both, at, found = (from_everyone(jnp.concatenate(lines), axis), 0, {})
    for k, line in zip(sequence, lines):
        share = both[:, at : at + len(line)].reshape(len(both), -1)
        found[k] = share[:, : leaves[k].size].reshape(-1, *leaves[k].shape)
        at += len(line)
    numbers = iter(range(len(leaves)))
    return jax.tree.map(lambda _: found[next(numbers)], shard)


def combined_pairwise(pieces, combine):
    while len(jax.tree.leaves(pieces)[0]) > 1:
        pieces = jax.vmap(combine)(
            *(jax.tree.map(lambda part: part[side::2], pieces) for side in (0, 1))
        )
    return jax.tree.map(lambda part: part[0], pieces)


def merged(shard, axis, combine):
    pieces = collected_together(shard, axis)
    return combined_pairwise(pieces, combine)


def joined_along(pieces, dim):
    lengths = list(pieces.shape[1:])
    lengths[dim] *= pieces.shape[0]
    return jnp.moveaxis(pieces, 0, dim).reshape(lengths)


def collect(shard, axis, dim):
    pieces = from_everyone(shard, axis)
    return joined_along(pieces, dim)


def token_mask(states, table, class_of):
    words = jnp.take(table, states, axis=0)
    shifts = lax.broadcasted_iota(jnp.int32, (1, 1, 32), 2)
    bit_values = jnp.bitwise_and(jnp.right_shift(words[:, :, None], shifts), 1)
    allowed_class = bit_values.reshape(words.shape[0], words.shape[1] * 32).astype(jnp.bfloat16)
    onehot = (
        lax.broadcasted_iota(jnp.int32, (allowed_class.shape[1], class_of.shape[0]), 0)
        == class_of[None, :]
    ).astype(jnp.bfloat16)
    return jnp.dot(allowed_class, onehot, preferred_element_type=jnp.float32) > 0.5


def masked_peak(logits, allowed):
    return jnp.max(jnp.where(allowed, logits, masked_floor), axis=1)


def weighted_sums(logits, allowed, peak):
    weights = jnp.where(allowed, jnp.exp(logits - peak[:, None]), 0.0)
    return (jnp.sum(weights, axis=1), jnp.sum(weights * logits, axis=1))


def combine(first, second):
    peak = jnp.maximum(first[0], second[0])
    scale_first = jnp.exp(first[0] - peak)
    scale_second = jnp.exp(second[0] - peak)
    return (
        peak,
        first[1] * scale_first + second[1] * scale_second,
        first[2] * scale_first + second[2] * scale_second,
    )


def finish(logits, allowed, peak, total, weighted):
    norm_log = peak + jnp.log(total)
    log_probs = jnp.where(allowed, logits - norm_log[:, None], 0.0)
    return (log_probs, norm_log - weighted / total)


def vocab_stats(logits, allowed):
    peak = masked_peak(logits, allowed)
    total, weighted = weighted_sums(logits, allowed, peak)
    peak, total, weighted = merged((peak, total, weighted), "vocab", combine)
    return (peak, total, weighted)


def on_device(hidden, head, states, class_of, table):
    all_rows = collect(hidden, "rows", 0)
    logits = jnp.dot(
        lax.all_gather(all_rows, "vocab", axis=1, tiled=True),
        head,
        preferred_element_type=jnp.float32,
    )
    group = lax.axis_index("rows")
    own_count = states.shape[0] // lax.axis_size("rows")
    own_logits = lax.all_to_all(logits, "rows", split_axis=0, concat_axis=1, tiled=True)
    own_states = lax.dynamic_slice_in_dim(states, group * own_count, own_count, 0)
    allowed = token_mask(own_states, table, class_of)
    peak, total, weighted = vocab_stats(own_logits, allowed)
    log_probs, entropy = finish(own_logits, allowed, peak, total, weighted)
    return (log_probs, entropy)


def solution(mesh):
    in_specs = (P("rows", "vocab"), P(None, ("vocab", "rows")), P(), P("vocab"), P())
    out_specs = (P("rows", "vocab"), P("rows"))
    return jax.shard_map(
        on_device, mesh=mesh, in_specs=in_specs, out_specs=out_specs, check_vma=False
    )
```

profile of v0, /device:TPU:1, one launch (start us, length us, event | category | flops | bytes accessed | tf_op | source)
XLA Modules:
  0.0 230.6 jit_solution(9323599690425845408)
XLA Ops:
  7.2 0.0 all-gather.2.cloned.1.call-start
  7.2 0.9 broadcast_in_dim.33
  8.1 24.9 %all_to_all.29 = bf16[8,128,256]{2,1,0:T(8,128)(2,1)} all-to-all(bf16[8,128,256]{2,1,0:T(8,128)(2,1)S(1)} %broadcast_in_dim.33), channel_id=1, replica_groups=mesh['rows'=8,'vocab'=32] {'rows'}, dimensions={0} | all-to-all | bytes 1048576 | tf_op jit(solution)/shard_map/all_to_all | solution.py:11
  33.0 0.0 all-gather.2.cloned.1.call-update
  33.0 84.8 %all-gather.2.cloned.1.call-done = bf16[1024,8192]{1,0:T(8,128)(2,1)} async-done(((bf16[1024,256]{1,0:T(8,128)(2,1)}), bf16[1024,8192]{1,0:T(8,128)(2,1)}) %all-gather.2.cloned.1.call-update) | async-done | bytes 16777232 | tf_op jit(solution)/shard_map/all_gather | solution.py:103
  117.8 15.4 %fusion.5 = f32[1024,594]{0,1:T(8,128)S(1)} fusion(bf16[1024,8192]{1,0:T(8,128)(2,1)} %all-gather.2.cloned.1.call-done, bf16[8192,594]{0,1:T(8,128)(2,1)} %param.6), kind=kOutput, calls=%fused_computation.42 | convolution fusion | flops 9965666304 | bytes 28942336 | tf_op jit(solution)/shard_map/dot_general | solution.py:102
  133.2 0.6 copy.19
  133.8 0.2 slice_bitcast_fusion
  133.9 1.9 copy.14
  135.8 6.7 %all-to-all-start.1 = ((f32[8,128,594]{1,2,0:T(8,128)}), f32[8,128,594]{1,2,0:T(8,128)S(1)}, u32[]{:S(2)}, u32[]{:S(2)}) async-start(f32[8,128,594]{1,2,0:T(8,128)} %copy.14), calls=%async_computation.1 | async-start | bytes 4915200 | tf_op jit(solution)/shard_map/all_to_all | solution.py:109
  142.5 0.1 shift_right_arithmetic.23
  142.6 1.2 copy.12
  143.8 0.8 compare_and_fusion
  144.6 1.2 gather_fusion
  145.8 0.9 broadcast_select_fusion
  146.8 0.1 fusion.3
  146.9 55.0 %all-to-all-done.1 = f32[8,128,594]{1,2,0:T(8,128)S(1)} async-done(((f32[8,128,594]{1,2,0:T(8,128)}), f32[8,128,594]{1,2,0:T(8,128)S(1)}, u32[]{:S(2)}, u32[]{:S(2)}) %all-to-all-start.1) | async-done | bytes 2433056 | tf_op jit(solution)/shard_map/all_to_all | solution.py:109
  202.0 0.0 copy-start
  202.0 1.4 copy-done
  203.4 0.0 copy-start.1
  203.4 1.8 all_to_all.24
  205.2 0.0 copy-done.1
  205.2 1.6 select_reduce_fusion
  206.8 0.7 fusion.1
  207.5 13.4 %all_to_all.30 = f32[32,3,128]{2,1,0:T(4,128)S(1)} all-to-all(f32[32,3,128]{2,1,0:T(4,128)S(1)} %broadcast_in_dim.36), channel_id=1, replica_groups=mesh['rows'=8,'vocab'=32] {'vocab'}, dimensions={0} | all-to-all | bytes 98304 | tf_op jit(solution)/shard_map/all_to_all | solution.py:11
  221.5 0.5 bitcast_subtract_fusion
  222.0 1.8 subtract_select_fusion
  (38 shorter events, 0.6 us)
Async XLA Ops:
  7.2 110.6 %all-gather.2.cloned.1.call-start = ((), (), s32[]{:S(2)}) async-start(), calls=%async_computation.3 | async-start | bytes 17301504 | tf_op jit(solution)/shard_map/all_gather | solution.py:103
  135.8 66.1 %all-to-all-start.1 = ((f32[8,128,594]{1,2,0:T(8,128)}), f32[8,128,594]{1,2,0:T(8,128)S(1)}, u32[]{:S(2)}, u32[]{:S(2)}) async-start(f32[8,128,594]{1,2,0:T(8,128)} %copy.14), calls=%async_computation.1 | async-start | bytes 4915200 | tf_op jit(solution)/shard_map/all_to_all | solution.py:109
  202.0 1.4 copy-start
  203.4 1.8 copy-start.1
Sparse Core Ops, SparseCore 0:
  33.1 84.6 all-gather.1
where the time goes:
time: 231 us
  waiting for transfers between devices  140 us (61%)
  blocking collectives  38.3 us (17%)
  matrix products  16.9 us (7%)
  between operations  14.2 us (6%)
  local copies, waits for them, and re-layouts  9.65 us (4%)
  starting transfers between devices  6.77 us (3%)
  other arithmetic  4.96 us (2%)
    all_gather x1, waiting for transfers between devices, on_device(): lax.all_gather(all_rows, 'vocab', axis=1, tiled=True)  84.8 us
    all_to_all x1, waiting for transfers between devices, on_device(): lax.all_to_all(logits, 'rows', split_axis=0, concat_axis=1, tiled=True)  55 us
    all_to_all x2, blocking collectives, from_everyone(): return lax.all_to_all(copies, axis, split_axis=0, concat_axis=0, tiled=True)  38.3 us
    dot_general x1, matrix products, on_device(): jnp.dot(lax.all_gather(all_rows, 'vocab', axis=1, tiled=True), head, pref...  15.4 us
    all_to_all x1, starting transfers between devices, on_device(): lax.all_to_all(logits, 'rows', split_axis=0, concat_axis=1, tiled=True)  6.73 us
  transfers between devices with their start and end apart: 2, of which 2 were waited for; matrix products, arithmetic and copies ran while one was open for 2% of the time, Pallas kernels for 0%

commit v1 on v0

--- a/solution.py
+++ b/solution.py
@@ -4,6 +4,13 @@
 from jax.sharding import PartitionSpec as P
 
 masked_floor = -1e30
+
+
+def register_stops_all_by_axis(xs):
+    carry_out = lax.psum(1, "vocab")
+    v_next = jnp.stack([xs] * carry_out, axis=0)
+    upper = lax.all_to_all(v_next, "vocab", split_axis=0, concat_axis=0)
+    return jnp.concatenate(upper, axis=1)
 
 
 def from_everyone(shard, axis):
@@ -99,11 +106,7 @@
 
 def on_device(hidden, head, states, class_of, table):
     all_rows = collect(hidden, "rows", 0)
-    logits = jnp.dot(
-        lax.all_gather(all_rows, "vocab", axis=1, tiled=True),
-        head,
-        preferred_element_type=jnp.float32,
-    )
+    logits = jnp.dot(register_stops_all_by_axis(all_rows), head, preferred_element_type=jnp.float32)
     group = lax.axis_index("rows")
     own_count = states.shape[0] // lax.axis_size("rows")
     own_logits = lax.all_to_all(logits, "rows", split_axis=0, concat_axis=1, tiled=True)

time: 231 us -> 381 us (1.65)
  blocking collectives: 38.3 us -> 234 us
  waiting for transfers between devices: 140 us -> 57.4 us
  local copies, waits for them, and re-layouts: 9.65 us -> 62.5 us
  between operations: 14.2 us -> 0.8 us
    all_to_all x0 -> x1, blocking collectives: none -> 195 us  [register_stops_all_by_axis(): upper = lax.all_to_all(v_next, 'vocab', split_axis=0, concat_axis=0)]
    all_gather x1 -> x0, waiting for transfers between devices: 84.8 us -> none  [on_device(): lax.all_gather(all_rows, 'vocab', axis=1, tiled=True)]
    reshape x0 -> x1, local copies, waits for them, and re-layouts: none -> 30.7 us  [register_stops_all_by_axis(): return jnp.concatenate(upper, axis=1)]
    dot_general x0 -> x1, local copies, waits for them, and re-layouts: none -> 25.6 us  [on_device(): jnp.dot(register_stops_all_by_axis(all_rows), head, preferred_element_typ...]
  transfers between devices with their start and end apart: 2 -> 1, of which waited for: 2 -> 1; matrix products, arithmetic and copies ran while one was open for 2% -> 1% of each run, Pallas kernels for 0% -> 0%
where the time goes in v1:
time: 381 us; the launch traced here: 380 us
  blocking collectives  234 us (61%)
  local copies, waits for them, and re-layouts  62.5 us (16%)
  waiting for transfers between devices  57.4 us (15%)
  matrix products  17.2 us (5%)
  starting transfers between devices  4.51 us (1%)
  other arithmetic  4.12 us (1%)
    all_to_all x1, blocking collectives, register_stops_all_by_axis(): upper = lax.all_to_all(v_next, 'vocab', split_axis=0, concat_axis=0)  195 us
    all_to_all x1, waiting for transfers between devices, on_device(): lax.all_to_all(logits, 'rows', split_axis=0, concat_axis=1, tiled=True)  57.4 us
    all_to_all x2, blocking collectives, from_everyone(): return lax.all_to_all(copies, axis, split_axis=0, concat_axis=0, tiled=True)  38.7 us
    reshape x1, local copies, waits for them, and re-layouts, register_stops_all_by_axis(): return jnp.concatenate(upper, axis=1)  30.7 us
    dot_general x1, local copies, waits for them, and re-layouts, on_device(): jnp.dot(register_stops_all_by_axis(all_rows), head, preferred_element_typ...  25.6 us
    dot_general x1, matrix products, on_device(): jnp.dot(register_stops_all_by_axis(all_rows), head, preferred_element_typ...  15.6 us
  transfers between devices with their start and end apart: 1, of which 1 were waited for; matrix products, arithmetic and copies ran while one was open for 1% of the time, Pallas kernels for 0%

profile of v1, /device:TPU:1, one launch (start us, length us, event | category | flops | bytes accessed | tf_op | source)
XLA Modules:
  0.0 380.2 jit_solution(3399105413083209618)
XLA Ops:
  0.6 0.9 broadcast_in_dim.33
  1.5 24.8 %all_to_all.31 = bf16[8,128,256]{2,1,0:T(8,128)(2,1)S(1)} all-to-all(bf16[8,128,256]{2,1,0:T(8,128)(2,1)S(1)} %broadcast_in_dim.33), channel_id=1, replica_groups=mesh['rows'=8,'vocab'=32] {'rows'}, dimensions={0} | all-to-all | bytes 1048576 | tf_op jit(solution)/shard_map/all_to_all | solution.py:18
  26.3 1.9 stack.3
  28.3 195.0 %all_to_all.32 = bf16[32,1024,256]{2,1,0:T(8,128)(2,1)S(1)} all-to-all(bf16[32,1024,256]{2,1,0:T(8,128)(2,1)S(1)} %stack.3), channel_id=1, replica_groups=mesh['rows'=8,'vocab'=32] {'vocab'}, dimensions={0} | all-to-all | bytes 33554432 | tf_op jit(solution)/shard_map/all_to_all | solution.py:12
  223.3 30.7 %copy.12 = bf16[1024,32,256]{2,1,0:T(8,128)(2,1)} copy(bf16[1024,32,256]{2,0,1:T(8,128)(2,1)S(1)} %bitcast.31) | data formatting | bytes 33554432 | tf_op jit(solution)/shard_map/reshape | solution.py:13
  254.0 25.6 %dot_general.9 = bf16[8,128,8192]{2,1,0:T(8,128)(2,1)} reshape(bf16[1024,32,256]{2,1,0:T(8,128)(2,1)} %copy.12) | data formatting | bytes 33554432 | tf_op jit(solution)/shard_map/dot_general | solution.py:109
  279.7 15.6 %fusion = f32[8,128,594]{1,2,0:T(8,128)} fusion(bf16[8,128,8192]{2,1,0:T(8,128)(2,1)} %dot_general.9, bf16[8192,594]{0,1:T(8,128)(2,1)} %param.6), kind=kOutput, calls=%fused_computation.1 | convolution fusion | flops 9965666304 | bytes 28942336 | tf_op jit(solution)/shard_map/dot_general | solution.py:109
  295.3 0.0 copy-start
  295.3 4.5 %all-to-all-start.2 = ((f32[8,128,594]{1,2,0:T(8,128)}), f32[8,128,594]{1,2,0:T(8,128)}, u32[]{:S(2)}, u32[]{:S(2)}) async-start(f32[8,128,594]{1,2,0:T(8,128)} %fusion), calls=%async_computation.2 | async-start | bytes 4915200 | tf_op jit(solution)/shard_map/all_to_all | solution.py:112
  299.8 0.1 shift_right_arithmetic.23
  299.9 0.0 copy-done
  299.9 0.3 copy.10
  300.2 0.8 compare_and_fusion
  301.0 0.6 gather_fusion
  301.7 0.1 broadcast_select_fusion
  301.8 0.1 fusion.5
  301.9 57.4 %all-to-all-done.2 = f32[8,128,594]{1,2,0:T(8,128)} async-done(((f32[8,128,594]{1,2,0:T(8,128)}), f32[8,128,594]{1,2,0:T(8,128)}, u32[]{:S(2)}, u32[]{:S(2)}) %all-to-all-start.2) | async-done | bytes 2433056 | tf_op jit(solution)/shard_map/all_to_all | solution.py:112
  359.3 0.0 copy-start.1
  359.3 1.8 all_to_all.25
  361.1 0.0 copy-done.1
  361.1 1.6 select_reduce_fusion
  362.6 0.7 fusion.3
  363.4 13.9 %all_to_all.33 = f32[32,3,128]{2,1,0:T(4,128)S(1)} all-to-all(f32[32,3,128]{2,1,0:T(4,128)S(1)} %broadcast_in_dim.36), channel_id=1, replica_groups=mesh['rows'=8,'vocab'=32] {'vocab'}, dimensions={0} | all-to-all | bytes 98304 | tf_op jit(solution)/shard_map/all_to_all | solution.py:18
  377.9 0.5 bitcast_subtract_fusion
  378.5 1.8 subtract_select_fusion
  (38 shorter events, 0.6 us)
Async XLA Ops:
  295.3 4.6 %copy-start = (s32[2048,8]{0,1:T(8,128)S(1)}, s32[2048,8]{0,1:T(8,128)}, u32[]{:S(2)}) copy-start(s32[2048,8]{0,1:T(8,128)} %param.9) | copy-start | bytes 196612
  295.3 64.0 %all-to-all-start.2 = ((f32[8,128,594]{1,2,0:T(8,128)}), f32[8,128,594]{1,2,0:T(8,128)}, u32[]{:S(2)}, u32[]{:S(2)}) async-start(f32[8,128,594]{1,2,0:T(8,128)} %fusion), calls=%async_computation.2 | async-start | bytes 4915200 | tf_op jit(solution)/shard_map/all_to_all | solution.py:112
  359.3 1.8 copy-start.1
